TPU v7x, 128 devices: a whole 4x4x4 slice. The times are simulated.
128 devices in a mesh: dp: 4 (over y), expert: 32 (over z, x, core).
Axes of the slice: x: 4, y: 4, z: 4, core: 2. Of those that a mesh axis runs over, the one named last changes fastest.
Arguments:
- hidden_in: bfloat16 [16384, 2880], P(('dp', 'expert')), may hold values from -6 to 6
- queries: bfloat16 [16384, 4096], P(('dp', 'expert')), may hold values from -50 to 50
- kv_pages: bfloat16 [2048, 128, 1024], P(('dp', 'expert')), may hold values from -4.5 to 4.5
- page_table: int32 [512, 4], P(('dp', 'expert')), may hold values from 0 to 15, as said below
- new_rows: int32 [512], P(('dp', 'expert')), may hold values from 1 to 125, as said below
- context: int32 [512], P(('dp', 'expert')), may hold values from 1 to 512, as said below
- sink_logits: float32 [64], replicated, may hold values from 0 to 8
- out_proj: bfloat16 [4096, 2880], P('dp'), may hold values from -0.09375 to 0.09375
- norm_gain: float32 [2880], replicated, may hold values from 0.1 to 1.9
- routes: int32 [16384, 4], P(('dp', 'expert')), may hold values from 0 to 31, all different within a row; in each aligned block of 128 rows (0 to 127, 128 to 255, ...) at most 20 rows name the same one
- route_weights: float32 [16384, 4], P(('dp', 'expert')), may hold values from 0.05 to 1
- gate_up: bfloat16 [32, 2, 2880, 2048], P('expert', None, None, 'dp'), may hold values from -0.109375 to 0.109375
- down_proj: bfloat16 [32, 2048, 2880], P('expert', 'dp'), may hold values from -0.125 to 0.125
Outputs:
- layer_out: bfloat16 [16384, 2880], P(('dp', 'expert'))
Inputs may be any that keep to these rules, and one draw needn't show every extreme that they name: `page_table`: each request's table row lists distinct pages of its own block of 16 pages; each block's table holds each of its page numbers once. The new_rows of one block of 4 requests sum to 128; one to three requests of each block have more than one. new_rows <= context; in every block some request has context 4 * 128. Within the 128 rows of one block, no expert is named by more than 20 routes; some expert reaches 20 in every draw.
All inputs are finite; a program needn't handle non-finite values.
Results may differ from a plain program's by a relative error of at most 0.015.
Values may be sent and summed in bfloat16 or wider, within the bound.
A program may use at most 128 MiB of HBM per device.

v0:
```python
import math

import jax
import jax.numpy as jnp
from jax import lax
from jax.sharding import PartitionSpec as P

QH = 64
KVH = 8
HD = 64
E = 32
CAP = 20


norm_eps = 1e-05


def attend_rows(queries, kv_pages, page_table, new_rows, context, sink_logits):
    row_count = queries.shape[0]
    req_count = new_rows.shape[0]
    page_count = kv_pages.shape[0]
    page_len = kv_pages.shape[1]
    per_req = page_table.shape[1]
    req_ends = jnp.cumsum(new_rows)
    row_index = jnp.arange(row_count, dtype=jnp.int32)
    owner_req = jnp.sum((row_index[:, None] >= req_ends[None, :]).astype(jnp.int32), axis=1)
    pick_req = (owner_req[:, None] == jnp.arange(req_count, dtype=jnp.int32)[None, :]).astype(
        jnp.int32
    )
    position = row_index + jnp.sum(pick_req * (context - req_ends)[None, :], axis=1)
    match = (
        page_table[:, :, None] == jnp.arange(page_count, dtype=jnp.int32)[None, None, :]
    ).astype(jnp.int32)
    order_in_req = (
        jnp.sum(match * (jnp.arange(per_req, dtype=jnp.int32) + 1)[None, :, None], axis=1) - 1
    )
    row_page_pos = jnp.sum(pick_req[:, :, None] * order_in_req[None, :, :], axis=1)
    offsets = jnp.arange(page_len, dtype=jnp.int32)
    slot_pos = row_page_pos[:, :, None] * page_len + offsets[None, None, :]
    visible = (row_page_pos[:, :, None] >= 0) & (slot_pos <= position[:, None, None])
    visible = visible.reshape(row_count, page_count * page_len)
    flat_cache = kv_pages.reshape(page_count * page_len, kv_pages.shape[2])
    group_size = QH // KVH

    def one_head(head_idx):
        kv_head = lax.dynamic_slice_in_dim(flat_cache, head_idx * 2 * HD, 2 * HD, 1)
        key_part = kv_head[:, :HD]
        value_part = kv_head[:, HD:]
        query_part = lax.dynamic_slice_in_dim(
            queries, head_idx * group_size * HD, group_size * HD, 1
        )
        query_part = query_part.reshape(row_count, group_size, HD)
        sink_part = lax.dynamic_slice_in_dim(sink_logits, head_idx * group_size, group_size, 0)
        scores = jnp.einsum(
            "rgd,sd->rgs", query_part, key_part, preferred_element_type=jnp.float32
        ) * (1.0 / math.sqrt(HD))
        scores = jnp.where(visible[:, None, :], scores, -jnp.inf)
        row_max = jnp.maximum(jnp.max(scores, axis=2), sink_part[None, :])
        weight = jnp.exp(scores - row_max[:, :, None])
        denom_sum = jnp.sum(weight, axis=2) + jnp.exp(sink_part[None, :] - row_max)
        probs_bf = (weight / denom_sum[:, :, None]).astype(jnp.bfloat16)
        return jnp.einsum(
            "rgs,sd->rgd", probs_bf, value_part, preferred_element_type=jnp.float32
        ).astype(jnp.bfloat16)

    head_parts = lax.map(one_head, jnp.arange(KVH, dtype=jnp.int32))
    return jnp.transpose(head_parts, (1, 0, 2, 3)).reshape(row_count, QH * HD)


def expert_terms(gathered_rows, gate_up, down_proj):
    local_count = gate_up.shape[0]
    senders = gathered_rows.shape[0] // local_count
    blocks = gathered_rows.reshape(
        senders, local_count, gathered_rows.shape[1], gathered_rows.shape[2]
    )
    gate_up_f = jnp.einsum("sjcd,jtdf->sjctf", blocks, gate_up, preferred_element_type=jnp.float32)
    gate_f = gate_up_f[:, :, :, 0, :]
    up_f = gate_up_f[:, :, :, 1, :]
    hidden = ((up_f + 1.0) * gate_f * jax.nn.sigmoid(1.702 * gate_f)).astype(jnp.bfloat16)
    down_f = jnp.einsum("sjcf,jfd->sjcd", hidden, down_proj, preferred_element_type=jnp.float32)
    return down_f.reshape(gathered_rows.shape)


def per_device(
    hidden_in,
    queries,
    kv_pages,
    page_table,
    new_rows,
    context,
    sink_logits,
    out_proj,
    norm_gain,
    routes,
    route_weights,
    gate_up,
    down_proj,
):
    row_count = hidden_in.shape[0]
    model_width = hidden_in.shape[1]
    attended = attend_rows(queries, kv_pages, page_table, new_rows, context, sink_logits)
    head_parts = lax.all_to_all(attended, "dp", split_axis=1, concat_axis=0, tiled=True)
    o_out = lax.psum_scatter(
        jnp.dot(head_parts, out_proj, preferred_element_type=jnp.float32).astype(jnp.bfloat16),
        "dp",
        scatter_dimension=0,
        tiled=True,
    ).astype(jnp.float32)
    mixed = (hidden_in.astype(jnp.float32) + o_out).astype(jnp.bfloat16)
    mixed_f = mixed.astype(jnp.float32)
    normed = (
        mixed_f
        * lax.rsqrt(jnp.mean(mixed_f * mixed_f, axis=1, keepdims=True) + norm_eps)
        * norm_gain
    ).astype(jnp.bfloat16)
    assign = routes.reshape(-1)
    onehot = (assign[:, None] == jnp.arange(E, dtype=jnp.int32)[None, :]).astype(jnp.int32)
    slot_index = jnp.sum((jnp.cumsum(onehot, axis=0) - onehot) * onehot, axis=1)
    source = jnp.arange(assign.shape[0], dtype=jnp.int32) // routes.shape[1]
    send_rows = (
        jnp.zeros((E, CAP, model_width), jnp.bfloat16).at[assign, slot_index].set(normed[source])
    )
    dp_count = lax.axis_size("dp")
    copies = jnp.broadcast_to(send_rows[None], (dp_count,) + send_rows.shape).reshape(
        dp_count * E, CAP, model_width
    )
    gathered_rows = lax.all_to_all(
        copies, ("dp", "expert"), split_axis=0, concat_axis=0, tiled=True
    )
    partials = expert_terms(gathered_rows, gate_up, down_proj).astype(jnp.bfloat16)
    returned_parts = lax.all_to_all(
        partials, ("dp", "expert"), split_axis=0, concat_axis=0, tiled=True
    )
    returned = jnp.sum(
        returned_parts.reshape(dp_count, E, CAP, model_width).astype(jnp.float32), axis=0
    )
    picked = returned[assign, slot_index]
    expert_mix = jnp.sum(
        (picked * route_weights.reshape(-1)[:, None]).reshape(
            row_count, routes.shape[1], model_width
        ),
        axis=1,
    )
    return (mixed_f + expert_mix).astype(jnp.bfloat16)


def solution(mesh):
    return jax.shard_map(
        per_device,
        mesh=mesh,
        in_specs=(
            P(("dp", "expert"), None),
            P(("dp", "expert"), None),
            P(("dp", "expert"), None, None),
            P(("dp", "expert"), None),
            P(("dp", "expert")),
            P(("dp", "expert")),
            P(),
            P("dp", None),
            P(),
            P(("dp", "expert"), None),
            P(("dp", "expert"), None),
            P("expert", None, None, "dp"),
            P("expert", "dp", None),
        ),
        out_specs=P(("dp", "expert"), None),
        check_vma=False,
    )
```

profile of v0, /device:TPU:34, one launch (start us, length us, event | category | flops | bytes accessed | tf_op | source)
XLA Modules:
  0.0 996.7 jit_solution(12575114656618149139)
XLA Ops:
  9.5 175.3 %while.13 = (s32[]{:T(128)}, bf16[8,128,8,64]{1,3,2,0:T(8,128)(2,1)}, s32[8]{0:T(128)S(1)}, bf16[128,4096]{1,0:T(8,128)(2,1)}, bf16[2048,1024]{1,0:T(8,128)(2,1)...) while((s32[]{:T(128)}, ...), condition=%wide.region_8.9_spmd.clone, body=%wide.region_5.8_spmd.clone.sunk | while | flops 562890752 | bytes 28627444 | solution.py:66
  13.6 5.9 fusion.52
  20.3 4.5 fusion.53
  24.9 6.5 fusion.54
  35.5 5.9 fusion.52
  42.2 4.5 fusion.53
  46.8 6.5 fusion.54
  57.4 5.9 fusion.52
  64.1 4.5 fusion.53
  68.7 6.5 fusion.54
  79.3 5.9 fusion.52
  86.0 4.5 fusion.53
  90.6 6.5 fusion.54
  101.2 5.9 fusion.52
  107.9 4.5 fusion.53
  112.5 6.5 fusion.54
  123.2 5.9 fusion.52
  129.8 4.5 fusion.53
  134.4 6.5 fusion.54
  145.1 5.9 fusion.52
  151.7 4.5 fusion.53
  156.4 6.5 fusion.54
  167.0 5.9 fusion.52
  173.7 4.5 fusion.53
  178.3 6.5 fusion.54
  184.8 19.8 %all_to_all.29 = bf16[128,4,1024]{0,2,1:T(8,128)(2,1)} all-to-all(bf16[128,4,1024]{0,2,1:T(8,128)(2,1)} %bitcast.113), channel_id=1, replica_groups=mesh['dp'=4,'expert'=32] {'dp'}, dimensions={1} | all-to-all | bytes 2097152 | tf_op jit(solution)/shard_map/all_to_all | solution.py:102
  204.6 2.3 copy.76
  206.9 7.9 convolution_convert_fusion.1
  214.8 4.6 copy.92
  221.5 35.2 %reduce-scatter.4.cloned.1.call-done = bf16[128,2880]{1,0:T(8,128)(2,1)} async-done(((bf16[512,2880]{1,0:T(8,128)(2,1)}), bf16[128,2880]{1,0:T(8,128)(2,1)}) %reduce-scatter.4.cloned.1.call-update) | async-done | bytes 737296
  260.6 2.7 fusion.31
  265.6 8.0 gather_fusion
  275.7 111.6 %scatter_fusion = bf16[32,20,2880]{2,0,1:T(8,128)(2,1)} fusion(bf16[32,20,2880]{2,0,1:T(8,128)(2,1)} %broadcast_in_dim.41, s32[512]{0:T(512)S(1)} %bitcast.106, bf16[512,2880]{1,0:T(8,128)(2,1)} %gather_fusion), kind=kCustom, calls=%fused_computation.2 | custom fusion | bytes 8851456 | tf_op jit(solution)/shard_map/scatter | solution.py:121
  387.3 3.9 broadcast_in_dim.42
  391.2 12.8 %copy.82 = bf16[128,20,2880]{2,1,0:T(8,128)(2,1)S(1)} copy(bf16[128,20,2880]{2,0,1:T(8,128)(2,1)S(1)} %bitcast.101) | data formatting | bytes 29491200 | tf_op jit(solution)/shard_map/reshape | solution.py:124
  404.0 210.1 %all_to_all.30 = bf16[128,20,2880]{2,1,0:T(8,128)(2,1)S(1)} all-to-all(bf16[128,20,2880]{2,1,0:T(8,128)(2,1)S(1)} %copy.82), channel_id=1, replica_groups=mesh['dp'=4,'expert'=32] {'dp','expert'}, dimensions={0} | all-to-all | bytes 29491200 | tf_op jit(solution)/shard_map/all_to_all | solution.py:127
  614.1 20.5 %fusion.20 = f32[128,1,20,2,512]{4,0,3,2,1:T(8,128)} fusion(bf16[1,2,2880,512]{3,2,1,0:T(8,128)(2,1)} %param.26, bf16[128,20,2880,1]{2,1,0,3:T(8,128)(2,1)S(1)} %bitcast.109), kind=kOutput, calls=%fused_computation.37 | convolution fusion | flops 15099494400 | bytes 31129600 | tf_op jit(solution)/shard_map/sjcd,jtdf->sjctf/dot_general | solution.py:76
  634.6 14.9 %convolution_convert_fusion = bf16[128,20,2880]{0,2,1:T(8,128)(2,1)} fusion(bf16[1,512,2880]{1,2,0:T(8,128)(2,1)S(1)} %copy-done, f32[128,1,20,2,512]{4,0,3,2,1:T(8,128)} %fusion.20), kind=kOutput, calls=%fused_computation.29 | convolution fusion | flops 7567605760 | bytes 28180480 | tf_op jit(solution)/shard_map/sjcf,jfd->sjcd/dot_general | solution.py:80
  649.5 22.2 %copy.84 = bf16[128,20,2880]{2,1,0:T(8,128)(2,1)} copy(bf16[128,20,2880]{0,2,1:T(8,128)(2,1)} %convolution_convert_fusion) | data formatting | bytes 29491200 | tf_op jit(solution)/shard_map/convert_element_type | solution.py:130
  671.7 9.1 all-to-all-start.2
  680.9 256.3 %all-to-all-done.2 = bf16[128,20,2880]{2,1,0:T(8,128)(2,1)} async-done(((bf16[128,20,2880]{2,1,0:T(8,128)(2,1)}), bf16[128,20,2880]{2,1,0:T(8,128)(2,1)}, u32[]{:S(2)}, u32[]{:S(2)}) %all-to-all-start.2) | async-done | bytes 14745632 | tf_op jit(solution)/shard_map/all_to_all | solution.py:131
  937.2 9.9 copy.85
  947.1 6.1 convert_reduce_fusion
  953.2 15.1 %gather_fusion.1 = f32[512,2880]{1,0:T(8,128)} fusion(f32[32,20,2880]{2,0,1:T(8,128)} %convert_reduce_fusion, s32[512]{0:T(512)S(1)} %bitcast.107), kind=kCustom, calls=%fused_computation.1 | custom fusion | bytes 11800576 | tf_op jit(solution)/shard_map/gather | solution.py:137
  968.2 7.6 gather.10
  975.9 8.1 multiply_reduce_fusion
  984.0 3.0 copy.87
  987.0 2.9 fusion.32
  (125 shorter events, 37.8 us)
Async XLA Ops:
  6.5 628.0 %copy-start = (bf16[1,512,2880]{1,2,0:T(8,128)(2,1)S(1)}, bf16[1,512,2880]{1,2,0:T(8,128)(2,1)}, u32[]{:S(2)}) copy-start(bf16[1,512,2880]{1,2,0:T(8,128)(2,1)} %param.27) | copy-start | bytes 8847364
  6.5 250.1 %reduce-scatter.4.cloned.1.call-start = ((), (), s32[]{:S(2)}) async-start(), calls=%async_computation.4 | async-start | bytes 3768320
  9.5 10.7 %copy-start.4 = (f32[64]{0:T(128)S(1)}, f32[64]{0:T(128)}, u32[]{:S(2)}) copy-start(f32[64]{0:T(128)} %get-tuple-element.295) | copy-start | bytes 772 | tf_op jit(solution)/shard_map/while
  31.4 10.6 %copy-start.4 = (f32[64]{0:T(128)S(1)}, f32[64]{0:T(128)}, u32[]{:S(2)}) copy-start(f32[64]{0:T(128)} %get-tuple-element.295) | copy-start | bytes 772 | tf_op jit(solution)/shard_map/while
  53.3 10.6 %copy-start.4 = (f32[64]{0:T(128)S(1)}, f32[64]{0:T(128)}, u32[]{:S(2)}) copy-start(f32[64]{0:T(128)} %get-tuple-element.295) | copy-start | bytes 772 | tf_op jit(solution)/shard_map/while
  75.2 10.6 %copy-start.4 = (f32[64]{0:T(128)S(1)}, f32[64]{0:T(128)}, u32[]{:S(2)}) copy-start(f32[64]{0:T(128)} %get-tuple-element.295) | copy-start | bytes 772 | tf_op jit(solution)/shard_map/while
  97.1 10.6 %copy-start.4 = (f32[64]{0:T(128)S(1)}, f32[64]{0:T(128)}, u32[]{:S(2)}) copy-start(f32[64]{0:T(128)} %get-tuple-element.295) | copy-start | bytes 772 | tf_op jit(solution)/shard_map/while
  119.0 10.6 %copy-start.4 = (f32[64]{0:T(128)S(1)}, f32[64]{0:T(128)}, u32[]{:S(2)}) copy-start(f32[64]{0:T(128)} %get-tuple-element.295) | copy-start | bytes 772 | tf_op jit(solution)/shard_map/while
  140.9 10.6 %copy-start.4 = (f32[64]{0:T(128)S(1)}, f32[64]{0:T(128)}, u32[]{:S(2)}) copy-start(f32[64]{0:T(128)} %get-tuple-element.295) | copy-start | bytes 772 | tf_op jit(solution)/shard_map/while
  162.9 10.6 %copy-start.4 = (f32[64]{0:T(128)S(1)}, f32[64]{0:T(128)}, u32[]{:S(2)}) copy-start(f32[64]{0:T(128)} %get-tuple-element.295) | copy-start | bytes 772 | tf_op jit(solution)/shard_map/while
  214.8 4.6 copy-start.2
  214.8 45.9 %copy-start.1 = (f32[2880]{0:T(1024)S(1)}, f32[2880]{0:T(1024)}, u32[]{:S(2)}) copy-start(f32[2880]{0:T(1024)} %param.23) | copy-start | bytes 34564
  671.7 9.1 copy-start.3
  671.7 265.5 %all-to-all-start.2 = ((bf16[128,20,2880]{2,1,0:T(8,128)(2,1)}), bf16[128,20,2880]{2,1,0:T(8,128)(2,1)}, u32[]{:S(2)}, u32[]{:S(2)}) async-start(bf16[128,20,2880]{2,1,0:T(8,128)(2,1)} %copy.84), calls=%async_computation.2 | async-start | bytes 36175872 | tf_op jit(solution)/shard_map/all_to_all | solution.py:131
Sparse Core Ops, SparseCore 0:
  219.5 37.0 reduce-scatter.3
where the time goes:
time: 1010 us; the launch traced here: 997 us
  waiting for transfers between devices  292 us (29%)
  blocking collectives  230 us (23%)
  local copies, waits for them, and re-layouts  224 us (22%)
  matrix products  142 us (14%)
  other arithmetic  71.1 us (7%)
  loops' own time  15.7 us (2%)
  between operations  13.5 us (1%)
    all_to_all x1, waiting for transfers between devices, per_device(): lax.all_to_all(partials, ('dp', 'expert'), split_axis=0, concat_axis=0, t...  256 us
    all_to_all x1, blocking collectives, per_device(): lax.all_to_all(copies, ('dp', 'expert'), split_axis=0, concat_axis=0, til...  210 us
    scatter x1, local copies, waits for them, and re-layouts, per_device(): jnp.zeros((E, CAP, model_width), jnp.bfloat16).at[assign, slot_index]  112 us
    dot_general x8, matrix products, one_head(): jnp.einsum('rgs,sd->rgd', probs_bf, value_part, preferred_element_type=jn...  51.9 us
    dot_general x8, matrix products, one_head(): jnp.einsum('rgd,sd->rgs', query_part, key_part, preferred_element_type=jn...  47 us
    reduce_sum x8, other arithmetic, one_head(): denom_sum = jnp.sum(weight, axis=2) + jnp.exp(sink_part[None, :] - row_max)  36.3 us
    unnamed x2, waiting for transfers between devices  35.2 us
    gather x2, local copies, waits for them, and re-layouts, per_device(): picked = returned[assign, slot_index]  22.7 us
  transfers between devices with their start and end apart: 2, of which 2 were waited for; matrix products, arithmetic and copies ran while one was open for 0% of the time, Pallas kernels for 0%

commit v1 on v0

v1 whole, which is shorter than its diff:
```python
import math

import jax
import jax.numpy as jnp
from jax import lax
from jax.experimental import pallas as pl
from jax.experimental.pallas import tpu as pltpu
from jax.sharding import PartitionSpec as P

QH = 64
KVH = 8
HD = 64
E = 32
CAP = 20
PAGE = 128
TILE = 16
GROUP = QH // KVH

norm_eps = 1e-05


def attend_kernel(table, new_rows, context, q_ref, kv_ref, sink_ref, out_ref):
    req_count = new_rows.shape[0]
    per_req = table.shape[1]
    lane = lax.broadcasted_iota(jnp.int32, (TILE, 2 * HD), 1)
    low = lane < HD
    sink = sink_ref[0]

    def tile_step(request, start, first_pos, chunk, pages):
        row0 = pl.multiple_of(chunk * TILE, TILE)
        rows = pl.ds(row0, TILE)
        parts = []
        for pair in range(GROUP // 2):
            q = q_ref[rows, pair * 2 * HD : (pair + 1) * 2 * HD].astype(jnp.float32) * (
                1.0 / math.sqrt(HD)
            )
            parts.append(jnp.where(low, q, 0.0))
            parts.append(jnp.where(low, pltpu.roll(q, HD, 1), 0.0))
        q_all = jnp.concatenate(parts, axis=0).astype(jnp.bfloat16)
        kv = jnp.concatenate([kv_ref[table[request, p]] for p in range(pages)], axis=0)
        scores = lax.dot_general(
            q_all, kv, (((1,), (1,)), ((), ())), preferred_element_type=jnp.float32
        )
        span = pages * PAGE
        row_in = lax.rem(lax.broadcasted_iota(jnp.int32, (GROUP * TILE, 1), 0), TILE)
        position = first_pos + (row0 + row_in - start)
        key = lax.broadcasted_iota(jnp.int32, (GROUP * TILE, span), 1)
        scores = jnp.where(key <= position, scores, -jnp.inf)
        row_max = jnp.maximum(jnp.max(scores, axis=1, keepdims=True), sink)
        weight = jnp.exp(scores - row_max)
        denom = jnp.sum(weight, axis=1, keepdims=True) + jnp.exp(sink - row_max)
        probs = (weight * (1.0 / denom)).astype(jnp.bfloat16)
        out = lax.dot_general(
            probs, kv, (((1,), (0,)), ((), ())), preferred_element_type=jnp.float32
        )
        row_id = row0 + lax.broadcasted_iota(jnp.int32, (TILE, 2 * HD), 0)
        mine = (row_id >= start) & (row_id < start + new_rows[request])
        for pair in range(GROUP // 2):
            even = out[2 * pair * TILE : (2 * pair + 1) * TILE]
            odd = out[(2 * pair + 1) * TILE : (2 * pair + 2) * TILE]
            both = jnp.where(low, pltpu.roll(even, HD, 1), odd)
            cols = slice(pair * 2 * HD, (pair + 1) * 2 * HD)
            old = out_ref[rows, cols].astype(jnp.float32)
            out_ref[rows, cols] = jnp.where(mine, both, old).astype(out_ref.dtype)

    start = 0
    for request in range(req_count):
        count = new_rows[request]
        first_pos = context[request] - count

        def body(chunk, carry, request=request, start=start, first_pos=first_pos, count=count):
            last_row = jnp.minimum(chunk * TILE + TILE, start + count) - 1
            pages = (first_pos + last_row - start) // PAGE + 1

            @pl.when(pages <= per_req // 2)
            def _():
                tile_step(request, start, first_pos, chunk, per_req // 2)

            @pl.when(pages > per_req // 2)
            def _():
                tile_step(request, start, first_pos, chunk, per_req)

            return carry

        lax.fori_loop(start // TILE, (start + count - 1) // TILE + 1, body, 0)
        start = start + count


def attend_rows(queries, kv_pages, page_table, new_rows, context, sink_logits):
    row_count = queries.shape[0]
    width = GROUP * HD
    sink_rows = jnp.repeat(sink_logits, TILE).reshape(KVH, GROUP * TILE, 1)
    return pl.pallas_call(
        attend_kernel,
        out_shape=jax.ShapeDtypeStruct(queries.shape, queries.dtype),
        grid_spec=pltpu.PrefetchScalarGridSpec(
            num_scalar_prefetch=3,
            grid=(KVH,),
            in_specs=[
                pl.BlockSpec((row_count, width), lambda h, *_: (0, h)),
                pl.BlockSpec(kv_pages.shape[:2] + (2 * HD,), lambda h, *_: (0, 0, h)),
                pl.BlockSpec((1, GROUP * TILE, 1), lambda h, *_: (h, 0, 0)),
            ],
            out_specs=pl.BlockSpec((row_count, width), lambda h, *_: (0, h)),
        ),
        name="attend",
    )(page_table, new_rows, context, queries, kv_pages, sink_rows)


def expert_terms(gathered_rows, gate_up, down_proj):
    gate_up_f = jnp.einsum("cd,tdf->tcf", gathered_rows, gate_up[0], preferred_element_type=jnp.float32)
    gate_f = gate_up_f[0]
    up_f = gate_up_f[1]
    hidden = ((up_f + 1.0) * gate_f * jax.nn.sigmoid(1.702 * gate_f)).astype(jnp.bfloat16)
    return jnp.dot(hidden, down_proj[0], preferred_element_type=jnp.float32)


def per_device(
    hidden_in,
    queries,
    kv_pages,
    page_table,
    new_rows,
    context,
    sink_logits,
    out_proj,
    norm_gain,
    routes,
    route_weights,
    gate_up,
    down_proj,
):
    row_count = hidden_in.shape[0]
    model_width = hidden_in.shape[1]
    attended = attend_rows(queries, kv_pages, page_table, new_rows, context, sink_logits)
    head_parts = lax.all_to_all(attended, "dp", split_axis=1, concat_axis=0, tiled=True)
    o_out = lax.psum_scatter(
        jnp.dot(head_parts, out_proj, preferred_element_type=jnp.float32).astype(jnp.bfloat16),
        "dp",
        scatter_dimension=0,
        tiled=True,
    ).astype(jnp.float32)
    mixed = (hidden_in.astype(jnp.float32) + o_out).astype(jnp.bfloat16)
    mixed_f = mixed.astype(jnp.float32)
    normed = (
        mixed_f
        * lax.rsqrt(jnp.mean(mixed_f * mixed_f, axis=1, keepdims=True) + norm_eps)
        * norm_gain
    ).astype(jnp.bfloat16)
    expert_ids = jnp.arange(E, dtype=jnp.int32)
    chosen = routes[:, :, None] == expert_ids[None, None, :]
    member = jnp.any(chosen, axis=1)
    order = jnp.arange(row_count, dtype=jnp.int32)
    before = (order[:, None] > order[None, :]).astype(jnp.bfloat16)
    rank = jnp.dot(before, member.astype(jnp.bfloat16), preferred_element_type=jnp.float32)
    rank = jnp.where(member, rank.astype(jnp.int32), -1)
    place = rank[:, :, None] == jnp.arange(CAP, dtype=jnp.int32)[None, None, :]
    weight_of = jnp.sum(jnp.where(chosen, route_weights[:, :, None], 0.0), axis=1)
    place_flat = place.reshape(row_count, E * CAP)
    send_rows = lax.dot_general(
        place_flat.astype(jnp.bfloat16),
        normed,
        (((0,), (0,)), ((), ())),
        preferred_element_type=jnp.float32,
    ).astype(jnp.bfloat16).reshape(E, CAP, model_width)
    spread = jnp.where(place, weight_of[:, :, None], 0.0).reshape(row_count, E * CAP)
    dp_count = lax.axis_size("dp")
    copies = jnp.broadcast_to(send_rows[None], (dp_count,) + send_rows.shape).reshape(
        dp_count * E, CAP, model_width
    )
    gathered_rows = lax.all_to_all(
        copies, ("dp", "expert"), split_axis=0, concat_axis=0, tiled=True
    )
    partials = expert_terms(
        gathered_rows.reshape(-1, model_width), gate_up, down_proj
    ).astype(jnp.bfloat16)
    returned = lax.all_to_all(
        partials.reshape(gathered_rows.shape),
        ("dp", "expert"),
        split_axis=0,
        concat_axis=0,
        tiled=True,
    ).reshape(dp_count * E * CAP, model_width)
    spread_bf = spread.astype(jnp.bfloat16)
    spread_low = (spread - spread_bf.astype(jnp.float32)).astype(jnp.bfloat16)
    expert_mix = jnp.dot(
        jnp.tile(spread_bf, (1, dp_count)), returned, preferred_element_type=jnp.float32
    ) + jnp.dot(jnp.tile(spread_low, (1, dp_count)), returned, preferred_element_type=jnp.float32)
    return (mixed_f + expert_mix).astype(jnp.bfloat16)


def solution(mesh):
    return jax.shard_map(
        per_device,
        mesh=mesh,
        in_specs=(
            P(("dp", "expert"), None),
            P(("dp", "expert"), None),
            P(("dp", "expert"), None, None),
            P(("dp", "expert"), None),
            P(("dp", "expert")),
            P(("dp", "expert")),
            P(),
            P("dp", None),
            P(),
            P(("dp", "expert"), None),
            P(("dp", "expert"), None),
            P("expert", None, None, "dp"),
            P("expert", "dp", None),
        ),
        out_specs=P(("dp", "expert"), None),
        check_vma=False,
    )
```

time: 1010 us -> 813 us (0.80)
  local copies, waits for them, and re-layouts: 224 us -> 117 us
  Pallas kernels: 0 us -> 72.6 us
  matrix products: 142 us -> 70.7 us
  other arithmetic: 71.1 us -> 2.94 us
  loops' own time: 15.7 us -> 0 us
    scatter x1 -> x0, local copies, waits for them, and re-layouts: 112 us -> none  [per_device(): jnp.zeros((E, CAP, model_width), jnp.bfloat16).at[assign, slot_index]]
    pallas_call x0 -> x1, Pallas kernels: none -> 72.6 us  [attend_rows(): pl.pallas_call(attend_kernel, out_shape=jax.ShapeDtypeStruct(queries.shap...]
    dot_general x18 -> x6, matrix products: 134 us -> 63.4 us  [the longest x1 22.2 us: expert_terms(): jnp.einsum('cd,tdf->tcf', gathered_rows, gate_up[0], preferred_element_ty...]
    reduce_sum x15 -> x1, other arithmetic: 51.6 us -> 0.01 us  [per_device(): jnp.sum(jnp.where(chosen, route_weights[:, :, None], 0.0), axis=1)]
    reshape x2 -> x3, local copies, waits for them, and re-layouts: 12.9 us -> 62.8 us  [the longest x1 21 us: per_device(): gathered_rows.reshape(-1, model_width)]
    gather x3 -> x0, local copies, waits for them, and re-layouts: 30.7 us -> none  [the longest x2 22.7 us: per_device(): picked = returned[assign, slot_index]]
    another operation x1 -> x0, loops' own time: 15.7 us -> none  [attend_rows(): head_parts = lax.map(one_head, jnp.arange(KVH, dtype=jnp.int32))]
    dynamic_slice x32 -> x0, local copies, waits for them, and re-layouts: 14 us -> none  [the longest x16 8.29 us: one_head(): lax.dynamic_slice_in_dim(queries, head_idx * group_size * HD, group_size...]
  transfers between devices with their start and end apart: 2 -> 2, of which waited for: 2 -> 2; matrix products, arithmetic and copies ran while one was open for 0% -> 1% of each run, Pallas kernels for 0% -> 0%
where the time goes in v1:
time: 813 us; the launch traced here: 799 us
  waiting for transfers between devices  284 us (35%)
  blocking collectives  229 us (28%)
  local copies, waits for them, and re-layouts  117 us (14%)
  Pallas kernels  72.6 us (9%)
  matrix products  70.7 us (9%)
  between operations  13.5 us (2%)
  starting transfers between devices  9.13 us (1%)
    all_to_all x1, waiting for transfers between devices, per_device(): lax.all_to_all(partials.reshape(gathered_rows.shape), ('dp', 'expert'), s...  252 us
    all_to_all x1, blocking collectives, per_device(): lax.all_to_all(copies, ('dp', 'expert'), split_axis=0, concat_axis=0, til...  210 us
    pallas_call x1, Pallas kernels, attend_rows(): pl.pallas_call(attend_kernel, out_shape=jax.ShapeDtypeStruct(queries.shap...  72.6 us
    unnamed x2, waiting for transfers between devices  32 us
    dot_general x1, matrix products, expert_terms(): jnp.einsum('cd,tdf->tcf', gathered_rows, gate_up[0], preferred_element_ty...  22.2 us
    reshape x1, local copies, waits for them, and re-layouts, per_device(): gathered_rows.reshape(-1, model_width)  21 us
    reshape x1, local copies, waits for them, and re-layouts, per_device(): returned = lax.all_to_all(partials.reshape(gathered_rows.shape), ('dp', '...  21 us
    reshape x1, local copies, waits for them, and re-layouts, per_device(): partials.reshape(gathered_rows.shape)  20.8 us
  transfers between devices with their start and end apart: 2, of which 2 were waited for; matrix products, arithmetic and copies ran while one was open for 1% of the time, Pallas kernels for 0%

profile of v1, /device:TPU:34, one launch (start us, length us, event | category | flops | bytes accessed | tf_op | source)
XLA Modules:
  0.0 799.1 jit_solution(10130368927221286207)
XLA Ops:
  6.5 0.0 copy-start
  6.5 0.0 reduce-scatter.4.cloned.1.call-start
  6.5 0.9 broadcast_in_dim.54
  7.4 0.1 broadcast_in_dim.55
  7.5 1.1 broadcast_in_dim.65.sink_ref
  8.6 72.6 %attend.1 = bf16[128,4096]{1,0:T(8,128)(2,1)} custom-call(s32[4,4]{1,0:T(4,128)} %table.1, s32[4]{0:T(128)} %new_rows.1, s32[4]{0:T(128)} %context.1, bf16[128,4096]{1,0:T(8,128)(2,1)} %q_ref.1, bf16[16,128,1024]{2,1,0:T(8,128)(2,1)} %kv_ref.1, f32[8,128,1]{2,1,0:T(8,128)} %broadcast_in_dim.65.sink_ref), custom_call_target="tpu_custom_call" | custom-call | tf_op jit(solution)/shard_map/attend/pallas_call | solution.py:93
  81.2 1.3 copy.50
  82.5 18.7 %all_to_all.29 = bf16[128,4,1024]{2,0,1:T(8,128)(2,1)S(1)} all-to-all(bf16[128,4,1024]{2,0,1:T(8,128)(2,1)S(1)} %bitcast.42), channel_id=1, replica_groups=mesh['dp'=4,'expert'=32] {'dp'}, dimensions={1} | all-to-all | bytes 2097152 | tf_op jit(solution)/shard_map/all_to_all | solution.py:136
  101.2 7.3 convolution_convert_fusion.2
  108.5 4.6 copy.44
  113.1 0.0 reduce-scatter.4.cloned.1.call-update
  113.1 0.0 copy-done.6
  113.2 0.0 copy-done.7
  113.2 0.8 broadcast_in_dim.60
  114.0 1.0 broadcast_in_dim.61
  115.0 0.1 fusion.18
  115.1 0.8 eq.44
  115.9 1.8 eq.45
  117.7 0.1 eq.47
  117.8 1.1 subtract_convert_fusion
  118.9 32.0 %reduce-scatter.4.cloned.1.call-done = bf16[128,2880]{1,0:T(8,128)(2,1)} async-done(((bf16[512,2880]{1,0:T(8,128)(2,1)}), bf16[128,2880]{1,0:T(8,128)(2,1)}) %reduce-scatter.4.cloned.1.call-update) | async-done | bytes 737296
  151.0 2.3 copy.45
  153.2 1.7 fusion.15
  155.0 0.0 copy-done.5
  155.0 4.3 convolution_convert_fusion.1
  159.3 6.2 copy.38
  165.5 6.4 broadcast_in_dim.63
  171.9 5.3 broadcast_in_dim.64
  177.2 210.1 %all_to_all.30 = bf16[128,20,2880]{2,1,0:T(8,128)(2,1)} all-to-all(bf16[128,20,2880]{2,1,0:T(8,128)(2,1)S(1)} %bitcast.41), channel_id=1, replica_groups=mesh['dp'=4,'expert'=32] {'dp','expert'}, dimensions={0} | all-to-all | bytes 29491200 | tf_op jit(solution)/shard_map/all_to_all | solution.py:171
  387.4 21.0 %reshape.100 = bf16[2560,2880]{1,0:T(8,128)(2,1)} reshape(bf16[128,20,2880]{2,1,0:T(8,128)(2,1)} %all_to_all.30) | data formatting | bytes 29491200 | tf_op jit(solution)/shard_map/reshape | solution.py:175
  408.3 22.2 %fusion.2 = f32[2,2560,512]{2,1,0:T(8,128)} fusion(bf16[2560,2880]{1,0:T(8,128)(2,1)} %reshape.100, bf16[1,2,2880,512]{3,2,1,0:T(8,128)(2,1)} %param.24), kind=kOutput, calls=%fused_computation.3 | convolution fusion | flops 15099494400 | bytes 31129600 | tf_op jit(solution)/shard_map/cd,tdf->tcf/dot_general | solution.py:111
  430.6 0.0 copy-done
  430.6 15.3 %convolution_convert_fusion = bf16[2560,2880]{0,1:T(8,128)(2,1)} fusion(bf16[1,512,2880]{1,2,0:T(8,128)(2,1)S(1)} %copy-done, f32[2,2560,512]{2,1,0:T(8,128)} %fusion.2), kind=kOutput, calls=%fused_computation | convolution fusion | flops 7567605760 | bytes 28180480 | tf_op jit(solution)/shard_map/dot_general | solution.py:115
  445.9 20.2 %copy.40 = bf16[2560,2880]{1,0:T(8,128)(2,1)} copy(bf16[2560,2880]{0,1:T(8,128)(2,1)} %convolution_convert_fusion) | data formatting | bytes 29491200 | tf_op jit(solution)/shard_map/convert_element_type | solution.py:176
  466.1 20.8 %reshape.101 = bf16[128,20,2880]{2,1,0:T(8,128)(2,1)} reshape(bf16[2560,2880]{1,0:T(8,128)(2,1)} %copy.40) | data formatting | bytes 29491200 | tf_op jit(solution)/shard_map/reshape | solution.py:178
  486.9 9.1 %all-to-all-start.2 = ((bf16[128,20,2880]{2,1,0:T(8,128)(2,1)}), bf16[128,20,2880]{2,1,0:T(8,128)(2,1)}, u32[]{:S(2)}, u32[]{:S(2)}) async-start(bf16[128,20,2880]{2,1,0:T(8,128)(2,1)} %reshape.101), calls=%async_computation.2 | async-start | bytes 36175872 | tf_op jit(solution)/shard_map/all_to_all | solution.py:177
  496.1 0.2 copy.37
  496.3 0.2 tile.8
  496.5 0.1 copy.47
  496.5 0.2 copy.41
  496.7 0.2 tile.20
  496.9 0.9 copy.48
  497.8 252.0 %all-to-all-done.2 = bf16[128,20,2880]{2,1,0:T(8,128)(2,1)} async-done(((bf16[128,20,2880]{2,1,0:T(8,128)(2,1)}), bf16[128,20,2880]{2,1,0:T(8,128)(2,1)}, u32[]{:S(2)}, u32[]{:S(2)}) %all-to-all-start.2) | async-done | bytes 14745632 | tf_op jit(solution)/shard_map/all_to_all | solution.py:177
  749.8 21.0 %reshape.102 = bf16[2560,2880]{1,0:T(8,128)(2,1)} reshape(bf16[128,20,2880]{2,1,0:T(8,128)(2,1)} %all-to-all-done.2) | data formatting | bytes 29491200 | tf_op jit(solution)/shard_map/reshape | solution.py:183
  770.8 10.5 %fusion.25 = f32[128,2880]{0,1:T(8,128)} fusion(bf16[128,2560]{1,0:T(8,128)(2,1)S(1)} %bitcast.44, bf16[2560,2880]{1,0:T(8,128)(2,1)} %reshape.102), kind=kOutput, calls=%fused_computation.38 | convolution fusion | flops 1887436800 | bytes 16875520 | tf_op jit(solution)/shard_map/dot_general | solution.py:186
  781.2 0.0 copy-done.2
  781.2 0.0 copy-done.3
  781.3 10.9 %fusion.10 = bf16[128,2880]{0,1:T(8,128)(2,1)} fusion(f32[128,2880]{0,1:T(8,128)} %fusion.25, bf16[128,2560]{1,0:T(8,128)(2,1)S(1)} %bitcast.45, bf16[2560,2880]{1,0:T(8,128)(2,1)} %reshape.102, bf16[128,2880]{0,1:T(8,128)(2,1)S(1)} %copy-done.2, bf16[128,2880]{0,1:T(8,128)(2,1)S(1)} %copy-done.3), kind=kOutput, calls=%fused_computation.13 | convolution fusion | flops 1890385920 | bytes 19087360 | tf_op jit(solution)/shard_map/dot_general | solution.py:188
  (14 shorter events, 0.1 us)
Async XLA Ops:
  6.5 424.0 %copy-start = (bf16[1,512,2880]{1,2,0:T(8,128)(2,1)S(1)}, bf16[1,512,2880]{1,2,0:T(8,128)(2,1)}, u32[]{:S(2)}) copy-start(bf16[1,512,2880]{1,2,0:T(8,128)(2,1)} %param.25) | copy-start | bytes 8847364
  6.5 144.4 %reduce-scatter.4.cloned.1.call-start = ((), (), s32[]{:S(2)}) async-start(), calls=%async_computation.4 | async-start | bytes 3768320
  108.5 4.6 copy-start.6
  108.5 4.6 copy-start.7
  113.1 41.9 %copy-start.5 = (f32[2880]{0:T(1024)S(1)}, f32[2880]{0:T(1024)}, u32[]{:S(2)}) copy-start(f32[2880]{0:T(1024)} %param.21) | copy-start | bytes 34564
  486.9 262.9 %all-to-all-start.2 = ((bf16[128,20,2880]{2,1,0:T(8,128)(2,1)}), bf16[128,20,2880]{2,1,0:T(8,128)(2,1)}, u32[]{:S(2)}, u32[]{:S(2)}) async-start(bf16[128,20,2880]{2,1,0:T(8,128)(2,1)} %reshape.101), calls=%async_computation.2 | async-start | bytes 36175872 | tf_op jit(solution)/shard_map/all_to_all | solution.py:177
  770.8 10.5 %copy-start.2 = (bf16[128,2880]{0,1:T(8,128)(2,1)S(1)}, bf16[128,2880]{0,1:T(8,128)(2,1)}, u32[]{:S(2)}) copy-start(bf16[128,2880]{0,1:T(8,128)(2,1)} %copy.45) | copy-start | bytes 2211844
  770.8 10.5 %copy-start.3 = (bf16[128,2880]{0,1:T(8,128)(2,1)S(1)}, bf16[128,2880]{0,1:T(8,128)(2,1)}, u32[]{:S(2)}) copy-start(bf16[128,2880]{0,1:T(8,128)(2,1)} %param.13) | copy-start | bytes 2211844
  770.8 10.5 %copy-start.4 = (bf16[16,8,4,640]{3,1,2,0:T(8,128)(2,1)S(1)}, bf16[16,8,4,640]{3,1,2,0:T(8,128)(2,1)}, u32[]{:S(2)}) copy-start(bf16[16,8,4,640]{3,1,2,0:T(8,128)(2,1)} %copy.48) | copy-start | bytes 1966084
  781.2 11.0 %copy-start.1 = (bf16[1,512,2880]{1,2,0:T(8,128)(2,1)S(1)}, bf16[1,512,2880]{1,2,0:T(8,128)(2,1)}, u32[]{:S(2)}) copy-start(bf16[1,512,2880]{1,2,0:T(8,128)(2,1)} %param.25) | copy-start | bytes 8847364
Sparse Core Ops, SparseCore 0:
  113.3 37.6 reduce-scatter.3
